TPU v7x, 32 devices: a whole 2x2x4 slice. The times are simulated.
32 devices in a mesh: rows: 4 (over y, x), cols: 8 (over z, core).
Axes of the slice: x: 2, y: 2, z: 4, core: 2. Of those that a mesh axis runs over, the one named last changes fastest.
Arguments:
- right_side: float32 [8192, 2048], P('rows', 'cols'), may hold values from -6 to 6
- inverse_blocks: float32 [8, 1024, 1024], P('rows', 'cols'), may hold values from -2 to 2, as said below
- coupling_blocks: float32 [8, 1024, 1024], P('rows', 'cols'), may hold values from -0.109375 to 0.109375
- prior_solution: float32 [1024, 2048], P(None, 'cols'), may hold values from -6 to 6
Outputs:
- solution: float32 [8192, 2048], P('rows', 'cols')
Inputs may be any that keep to these rules, and one draw needn't show every extreme that they name: inverse_blocks holds the inverses of well conditioned diagonal blocks of the factor.
All inputs are finite; a program needn't handle non-finite values.
Results may differ from a plain program's by a relative error of at most 0.00013.
Values sent between devices are 32-bit elements; how exact they have to be, the bound alone decides.
No kernel may reach another device: no remote copies, remote signals or barrier semaphores. Data moves between devices by JAX's collectives and lax.ppermute only.
A program may use at most 128 MiB of HBM per device.

v0:
```python
import jax
import jax.numpy as jnp
from jax import lax
from jax.sharding import PartitionSpec as P

HIGHEST_PRECISION = lax.Precision.HIGHEST


def shifted(shard, axis, by):
    devices = lax.axis_size(axis)
    pairs = [(i, i + by) for i in range(devices) if 0 <= i + by < devices]
    return lax.ppermute(shard, axis, pairs)


def local(right_side, inverse_blocks, coupling_blocks, prior_solution):
    count_blocks = inverse_blocks.shape[0]
    block_rows = inverse_blocks.shape[2]
    col_width = right_side.shape[1]
    group_count = lax.axis_size("rows")
    row_group = lax.axis_index("rows")
    blocks = right_side.reshape(count_blocks, block_rows, col_width)
    inverse_full, coupling_full = (
        lax.all_gather(inverse_blocks, "cols", axis=1, tiled=True),
        lax.all_gather(coupling_blocks, "cols", axis=1, tiled=True),
    )
    pieces = 1
    wave_cols = col_width // pieces
    solution = jnp.zeros((count_blocks, block_rows, col_width), jnp.float32)
    incoming = jnp.zeros((block_rows, wave_cols), jnp.float32)
    step_count = group_count + pieces - 1
    for step_index in range(step_count):
        wave_index = step_index - row_group
        active = jnp.logical_and(wave_index >= 0, wave_index < pieces)
        previous = jnp.where(row_group == 0, prior_solution, incoming)
        results = []
        for block_index in range(count_blocks):
            local_rhs = blocks[block_index]
            pushed = local_rhs - jnp.dot(
                coupling_full[block_index],
                previous,
                precision=HIGHEST_PRECISION,
                preferred_element_type=jnp.float32,
            )
            previous = jnp.dot(
                inverse_full[block_index],
                pushed,
                precision=HIGHEST_PRECISION,
                preferred_element_type=jnp.float32,
            )
            results.append(previous)
        stacked = jnp.stack(results)
        current = solution
        solution = jnp.where(active, stacked, current)
        if step_index + 1 < step_count:
            incoming = shifted(previous, "rows", 1)
    return solution.reshape(count_blocks * block_rows, col_width)


def solution(mesh):
    placed = (P("rows", "cols"), P("rows", "cols", None), P("rows", "cols", None), P(None, "cols"))
    return jax.shard_map(
        local, mesh=mesh, in_specs=placed, out_specs=P("rows", "cols"), check_vma=False
    )
```

profile of v0, /device:TPU:4, one launch (start us, length us, event | category | flops | bytes accessed | tf_op | source)
XLA Modules:
  0.0 361.7 jit_solution(14020077271531396193)
XLA Ops:
  9.6 82.6 %all-gather.3.cloned.1.call-done = f32[2,1024,1024]{2,1,0:T(8,128)} async-done(((f32[2,128,1024]{2,1,0:T(8,128)}), f32[2,1024,1024]{2,1,0:T(8,128)}) %all-gather.3.cloned.1.call-update) | async-done | bytes 8388624 | tf_op jit(solution)/shard_map/all_gather | solution.py:24
  92.2 6.6 %fusion.26 = f32[1024,256]{1,0:T(8,128)} fusion(f32[2,1024,1024]{2,1,0:T(8,128)} %all-gather.3.cloned.1.call-done, f32[1024,256]{0,1:T(8,128)S(1)} %copy.12, f32[2048,256]{1,0:T(8,128)S(1)} %copy-done.1, pred[]{:T(512)S(6)} %eq.2), kind=kOutput, calls=%fused_computation.34 | convolution fusion | flops 3221749760 | bytes 7340033 | tf_op jit(solution)/shard_map/dot_general | solution.py:38
  98.8 75.5 %all-gather.5.cloned.1.call-done = f32[2,1024,1024]{2,1,0:T(8,128)} async-done(((f32[2,128,1024]{2,1,0:T(8,128)}), f32[2,1024,1024]{2,1,0:T(8,128)}) %all-gather.5.cloned.1.call-update) | async-done | bytes 8388624 | tf_op jit(solution)/shard_map/all_gather | solution.py:23
  174.4 9.1 %fusion.7 = f32[256,1024]{1,0:T(8,128)S(1)} fusion(f32[1024,256]{1,0:T(8,128)} %fusion.26, f32[2,1024,1024]{2,1,0:T(8,128)} %all-gather.5.cloned.1.call-done), kind=kOutput, calls=%fused_computation.11 | convolution fusion | flops 3221225472 | bytes 6291456 | tf_op jit(solution)/shard_map/dot_general | solution.py:44
  183.5 6.3 %fusion.18 = f32[1024,256]{1,0:T(8,128)S(1)} fusion(f32[256,1024]{1,0:T(8,128)S(1)} %fusion.7, f32[2,1024,1024]{2,1,0:T(8,128)} %all-gather.3.cloned.1.call-done, f32[2048,256]{1,0:T(8,128)S(1)} %copy-done.1), kind=kOutput, calls=%fused_computation.26 | convolution fusion | flops 3221487616 | bytes 7340032 | tf_op jit(solution)/shard_map/dot_general | solution.py:38
  189.9 7.1 %fusion.15 = f32[256,1024]{1,0:T(8,128)S(1)} fusion(f32[1024,256]{1,0:T(8,128)S(1)} %fusion.18, f32[2,1024,1024]{2,1,0:T(8,128)S(1)} %copy-done), kind=kOutput, calls=%fused_computation.19 | convolution fusion | flops 3221225472 | bytes 6291456 | tf_op jit(solution)/shard_map/dot_general | solution.py:44
  196.9 3.5 collective-permute-start
  200.5 24.5 %collective-permute-done = f32[1024,256]{0,1:T(8,128)S(1)} collective-permute-done((f32[1024,256]{0,1:T(8,128)S(1)}, f32[1024,256]{0,1:T(8,128)S(1)}, u32[]{:S(2)}, u32[]{:S(2)}) %collective-permute-start) | collective-permute-done | bytes 1048608 | tf_op jit(solution)/shard_map/ppermute | solution.py:12
  225.0 3.5 fusion.28
  228.6 7.1 %fusion.6 = f32[256,1024]{1,0:T(8,128)S(1)} fusion(f32[1024,256]{1,0:T(8,128)S(1)} %fusion.28, f32[2,1024,1024]{2,1,0:T(8,128)S(1)} %copy-done), kind=kOutput, calls=%fused_computation.10 | convolution fusion | flops 3221225472 | bytes 6291456 | tf_op jit(solution)/shard_map/dot_general | solution.py:44
  235.6 3.7 %fusion.20 = f32[1024,256]{1,0:T(8,128)S(1)} fusion(f32[256,1024]{1,0:T(8,128)S(1)} %fusion.6, f32[2,1024,1024]{2,1,0:T(8,128)S(1)} %bitcast.129, f32[2048,256]{1,0:T(8,128)S(1)} %copy-done.1), kind=kOutput, calls=%fused_computation.28 | convolution fusion | flops 3221487616 | bytes 7340032 | tf_op jit(solution)/shard_map/dot_general | solution.py:38
  239.4 7.1 %fusion.14 = f32[256,1024]{1,0:T(8,128)S(1)} fusion(f32[1024,256]{1,0:T(8,128)S(1)} %fusion.20, f32[2,1024,1024]{2,1,0:T(8,128)S(1)} %copy-done), kind=kOutput, calls=%fused_computation.18 | convolution fusion | flops 3221225472 | bytes 6291456 | tf_op jit(solution)/shard_map/dot_general | solution.py:44
  246.4 2.9 collective-permute-start.1
  249.3 24.3 %collective-permute-done.1 = f32[1024,256]{0,1:T(8,128)S(1)} collective-permute-done((f32[1024,256]{0,1:T(8,128)S(1)}, f32[1024,256]{0,1:T(8,128)S(1)}, u32[]{:S(2)}, u32[]{:S(2)}) %collective-permute-start.1) | collective-permute-done | bytes 1048608 | tf_op jit(solution)/shard_map/ppermute | solution.py:12
  273.7 3.5 fusion.30
  277.2 7.1 %fusion.5 = f32[256,1024]{1,0:T(8,128)S(1)} fusion(f32[1024,256]{1,0:T(8,128)S(1)} %fusion.30, f32[2,1024,1024]{2,1,0:T(8,128)S(1)} %copy-done), kind=kOutput, calls=%fused_computation.9 | convolution fusion | flops 3221225472 | bytes 6291456 | tf_op jit(solution)/shard_map/dot_general | solution.py:44
  284.3 3.7 %fusion.22 = f32[1024,256]{1,0:T(8,128)S(1)} fusion(f32[256,1024]{1,0:T(8,128)S(1)} %fusion.5, f32[2,1024,1024]{2,1,0:T(8,128)S(1)} %bitcast.129, f32[2048,256]{1,0:T(8,128)S(1)} %copy-done.1), kind=kOutput, calls=%fused_computation.30 | convolution fusion | flops 3221487616 | bytes 7340032 | tf_op jit(solution)/shard_map/dot_general | solution.py:38
  287.9 8.0 %fusion.13 = f32[256,1024]{1,0:T(8,128)} fusion(f32[1024,256]{1,0:T(8,128)S(1)} %fusion.22, f32[2,1024,1024]{2,1,0:T(8,128)S(1)} %copy-done), kind=kOutput, calls=%fused_computation.17 | convolution fusion | flops 3221225472 | bytes 6291456 | tf_op jit(solution)/shard_map/dot_general | solution.py:44
  298.1 24.5 %collective-permute-done.2 = f32[1024,256]{0,1:T(8,128)} collective-permute-done((f32[1024,256]{0,1:T(8,128)}, f32[1024,256]{0,1:T(8,128)}, u32[]{:S(2)}, u32[]{:S(2)}) %collective-permute-start.2) | collective-permute-done | bytes 1048608 | tf_op jit(solution)/shard_map/ppermute | solution.py:12
  322.7 5.8 %fusion.32 = f32[1024,256]{1,0:T(8,128)S(1)} fusion(f32[2,1024,1024]{2,1,0:T(8,128)} %all-gather.3.cloned.1.call-done, f32[1024,256]{0,1:T(8,128)S(1)} %copy.12, f32[1024,256]{0,1:T(8,128)} %collective-permute-done.2, f32[2048,256]{1,0:T(8,128)S(1)} %copy-done.1, pred[]{:T(512)S(6)} %eq.2), kind=kOutput, calls=%fused_computation.40 | convolution fusion | flops 3221749760 | bytes 8388609 | tf_op jit(solution)/shard_map/dot_general | solution.py:38
  328.4 9.4 %fusion.4 = f32[256,1024]{1,0:T(8,128)S(1)} fusion(f32[1024,256]{1,0:T(8,128)S(1)} %fusion.32, f32[2,1024,1024]{2,1,0:T(8,128)} %all-gather.5.cloned.1.call-done), kind=kOutput, calls=%fused_computation.8 | convolution fusion | flops 3221225472 | bytes 6291456 | tf_op jit(solution)/shard_map/dot_general | solution.py:44
  337.8 5.6 %fusion.24 = f32[1024,256]{1,0:T(8,128)S(1)} fusion(f32[256,1024]{1,0:T(8,128)S(1)} %fusion.4, f32[2,1024,1024]{2,1,0:T(8,128)} %all-gather.3.cloned.1.call-done, f32[2048,256]{1,0:T(8,128)S(1)} %copy-done.1), kind=kOutput, calls=%fused_computation.32 | convolution fusion | flops 3221487616 | bytes 7340032 | tf_op jit(solution)/shard_map/dot_general | solution.py:38
  343.5 7.1 %fusion.16 = f32[1,1024,256]{1,2,0:T(8,128)S(1)} fusion(f32[1024,256]{1,0:T(8,128)S(1)} %fusion.24, f32[2,1024,1024]{2,1,0:T(8,128)S(1)} %bitcast.131), kind=kOutput, calls=%fused_computation.24 | convolution fusion | flops 3221225472 | bytes 6291456 | tf_op jit(solution)/shard_map/dot_general | solution.py:44
  350.6 2.2 maximum_select_fusion
  (41 shorter events, 7.0 us)
Async XLA Ops:
  6.5 85.7 %copy-start.1 = (f32[2048,256]{1,0:T(8,128)S(1)}, f32[2048,256]{1,0:T(8,128)}, u32[]{:S(2)}) copy-start(f32[2048,256]{1,0:T(8,128)} %param.4) | copy-start | bytes 6291460
  6.5 85.7 %all-gather.3.cloned.1.call-start = ((), (), s32[]{:S(2)}) async-start(), calls=%async_computation | async-start | bytes 9437184 | tf_op jit(solution)/shard_map/all_gather | solution.py:24
  7.3 167.1 %all-gather.5.cloned.1.call-start = ((), (), s32[]{:S(2)}) async-start(), calls=%async_computation.1 | async-start | bytes 9437184 | tf_op jit(solution)/shard_map/all_gather | solution.py:23
  174.4 15.5 %copy-start = (f32[2,1024,1024]{2,1,0:T(8,128)S(1)}, f32[2,1024,1024]{2,1,0:T(8,128)}, u32[]{:S(2)}) copy-start(f32[2,1024,1024]{2,1,0:T(8,128)} %all-gather.5.cloned.1.call-done) | copy-start | bytes 25165828
  174.4 50.7 %slice-start = ((s8[8388608]{0:T(1024)(128)(4,1)}), s8[4194304]{0:T(1024)(128)(4,1)S(1)}, s32[]{:S(2)}) async-start(s8[8388608]{0:T(1024)(128)(4,1)} %bitcast.128), calls=%async_computation.2 | async-start | bytes 8388608
  183.5 13.4 %copy-start.2 = (f32[256,1024]{1,0:T(8,128)}, f32[256,1024]{1,0:T(8,128)S(1)}, u32[]{:S(2)}) copy-start(f32[256,1024]{1,0:T(8,128)S(1)} %fusion.7) | copy-start | bytes 3145732
  183.5 41.5 %slice-start.1 = ((s8[8388608]{0:T(1024)(128)(4,1)}), s8[4194304]{0:T(1024)(128)(4,1)S(1)}, s32[]{:S(2)}) async-start(s8[8388608]{0:T(1024)(128)(4,1)} %bitcast.128), calls=%async_computation.3 | async-start | bytes 8388608
  196.9 31.6 %copy-start.8 = (f32[256,1024]{1,0:T(8,128)}, f32[256,1024]{1,0:T(8,128)S(1)}, u32[]{:S(2)}) copy-start(f32[256,1024]{1,0:T(8,128)S(1)} %fusion.15) | copy-start | bytes 3145732
  196.9 28.1 %collective-permute-start = (f32[1024,256]{0,1:T(8,128)S(1)}, f32[1024,256]{0,1:T(8,128)S(1)}, u32[]{:S(2)}, u32[]{:S(2)}) collective-permute-start(f32[1024,256]{0,1:T(8,128)S(1)} %bitcast.136), channel_id=1, source_target_pairs={{0,8},{8,16},{16,24},{1,9},{9,17},{17,25},{2,10},{10,18},{18,26},{... | collective-permute-start | bytes 3145736 | tf_op jit(solution)/shard_map/ppermute | solution.py:12
  235.6 10.8 %copy-start.4 = (f32[256,1024]{1,0:T(8,128)}, f32[256,1024]{1,0:T(8,128)S(1)}, u32[]{:S(2)}) copy-start(f32[256,1024]{1,0:T(8,128)S(1)} %fusion.6) | copy-start | bytes 3145732
  246.4 30.7 %copy-start.10 = (f32[256,1024]{1,0:T(8,128)}, f32[256,1024]{1,0:T(8,128)S(1)}, u32[]{:S(2)}) copy-start(f32[256,1024]{1,0:T(8,128)S(1)} %fusion.14) | copy-start | bytes 3145732
  246.4 27.2 %collective-permute-start.1 = (f32[1024,256]{0,1:T(8,128)S(1)}, f32[1024,256]{0,1:T(8,128)S(1)}, u32[]{:S(2)}, u32[]{:S(2)}) collective-permute-start(f32[1024,256]{0,1:T(8,128)S(1)} %bitcast.138), channel_id=1, source_target_pairs={{0,8},{8,16},{16,24},{1,9},{9,17},{17,25},{2,10},{10,18},{18,26},{... | collective-permute-start | bytes 3145736 | tf_op jit(solution)/shard_map/ppermute | solution.py:12
  284.3 11.7 %copy-start.6 = (f32[256,1024]{1,0:T(8,128)}, f32[256,1024]{1,0:T(8,128)S(1)}, u32[]{:S(2)}) copy-start(f32[256,1024]{1,0:T(8,128)S(1)} %fusion.5) | copy-start | bytes 3145732
  296.0 26.7 %collective-permute-start.2 = (f32[1024,256]{0,1:T(8,128)}, f32[1024,256]{0,1:T(8,128)}, u32[]{:S(2)}, u32[]{:S(2)}) collective-permute-start(f32[1024,256]{0,1:T(8,128)} %bitcast.12), channel_id=1, source_target_pairs={{0,8},{8,16},{16,24},{1,9},{9,17},{17,25},{2,10},{10,18},{18,26},{... | collective-permute-start | bytes 3145736 | tf_op jit(solution)/shard_map/ppermute | solution.py:12
  322.7 20.7 %slice-start.2 = ((s8[8388608]{0:T(1024)(128)(4,1)}), s8[4194304]{0:T(1024)(128)(4,1)S(1)}, s32[]{:S(2)}) async-start(s8[8388608]{0:T(1024)(128)(4,1)} %bitcast.130), calls=%async_computation.4 | async-start | bytes 8388608
  328.4 15.0 %slice-start.3 = ((s8[8388608]{0:T(1024)(128)(4,1)}), s8[4194304]{0:T(1024)(128)(4,1)S(1)}, s32[]{:S(2)}) async-start(s8[8388608]{0:T(1024)(128)(4,1)} %bitcast.130), calls=%async_computation.5 | async-start | bytes 8388608
  343.4 7.1 %copy-start.3 = (f32[256,1024]{1,0:T(8,128)S(1)}, f32[256,1024]{1,0:T(8,128)}, u32[]{:S(2)}) copy-start(f32[256,1024]{1,0:T(8,128)} %copy-done.2) | copy-start | bytes 3145732
  343.4 7.1 %copy-start.5 = (f32[256,1024]{1,0:T(8,128)S(1)}, f32[256,1024]{1,0:T(8,128)}, u32[]{:S(2)}) copy-start(f32[256,1024]{1,0:T(8,128)} %copy-done.4) | copy-start | bytes 3145732
  343.4 7.1 %copy-start.7 = (f32[256,1024]{1,0:T(8,128)S(1)}, f32[256,1024]{1,0:T(8,128)}, u32[]{:S(2)}) copy-start(f32[256,1024]{1,0:T(8,128)} %copy-done.6) | copy-start | bytes 3145732
  343.4 7.1 %copy-start.9 = (f32[256,1024]{1,0:T(8,128)S(1)}, f32[256,1024]{1,0:T(8,128)}, u32[]{:S(2)}) copy-start(f32[256,1024]{1,0:T(8,128)} %copy-done.8) | copy-start | bytes 3145732
  343.5 7.1 %copy-start.11 = (f32[256,1024]{1,0:T(8,128)S(1)}, f32[256,1024]{1,0:T(8,128)}, u32[]{:S(2)}) copy-start(f32[256,1024]{1,0:T(8,128)} %copy-done.10) | copy-start | bytes 3145732
Sparse Core Ops, SparseCore 0:
  8.9 83.2 all-gather.2
  93.8 80.5 all-gather.4
where the time goes:
time: 369 us; the launch traced here: 362 us
  waiting for transfers between devices  233 us (63%)
  matrix products  100 us (27%)
  between operations  14 us (4%)
  starting transfers between devices  8.59 us (2%)
    all_gather x1, waiting for transfers between devices, local(): lax.all_gather(coupling_blocks, 'cols', axis=1, tiled=True)  82.6 us
    all_gather x1, waiting for transfers between devices, local(): lax.all_gather(inverse_blocks, 'cols', axis=1, tiled=True)  75.5 us
    ppermute x3, waiting for transfers between devices, shifted(): return lax.ppermute(shard, axis, pairs)  73.4 us
    dot_general x8, matrix products, local(): jnp.dot(inverse_full[block_index], pushed, precision=HIGHEST_PRECISION, p...  61.8 us
    dot_general x8, matrix products, local(): jnp.dot(coupling_full[block_index], previous, precision=HIGHEST_PRECISION...  38.6 us
    ppermute x3, starting transfers between devices, shifted(): return lax.ppermute(shard, axis, pairs)  8.55 us
  transfers between devices with their start and end apart: 5, of which 5 were waited for; matrix products, arithmetic and copies ran while one was open for 2% of the time, Pallas kernels for 0%

commit v1 on v0

--- a/solution.py
+++ b/solution.py
@@ -1,9 +1,20 @@
+import functools
 import jax
 import jax.numpy as jnp
 from jax import lax
 from jax.sharding import PartitionSpec as P
 
 HIGHEST_PRECISION = lax.Precision.HIGHEST
+
+
+def place_sources_all(message, on_dim):
+    n_peers_all = lax.axis_size("cols")
+    xs_all = tuple((n_peers_all if idx == on_dim else 1 for idx in range(message.ndim)))
+    x_now = jnp.tile(message, xs_all)
+    return lax.all_to_all(x_now, "cols", split_axis=on_dim, concat_axis=on_dim, tiled=True)
+
+
+compute_the_samples = functools.partial(place_sources_all, on_dim=1)
 
 
 def shifted(shard, axis, by):
@@ -21,7 +32,7 @@
     blocks = right_side.reshape(count_blocks, block_rows, col_width)
     inverse_full, coupling_full = (
         lax.all_gather(inverse_blocks, "cols", axis=1, tiled=True),
-        lax.all_gather(coupling_blocks, "cols", axis=1, tiled=True),
+        compute_the_samples(coupling_blocks),
     )
     pieces = 1
     wave_cols = col_width // pieces

time: 369 us -> 456 us (1.24)
  waiting for transfers between devices: 233 us -> 318 us
  local copies, waits for them, and re-layouts: 3.44 us -> 27.7 us
  matrix products: 100 us -> 76.7 us
  starting transfers between devices: 8.59 us -> 13.2 us
    all_to_all x0 -> x1, waiting for transfers between devices: none -> 246 us  [place_sources_all(): lax.all_to_all(x_now, 'cols', split_axis=on_dim, concat_axis=on_dim, tile...]
    all_gather x1 -> x0, waiting for transfers between devices: 82.6 us -> none  [local(): lax.all_gather(coupling_blocks, 'cols', axis=1, tiled=True)]
    all_gather x1, waiting for transfers between devices: 75.5 us -> 0.01 us  [local(): lax.all_gather(inverse_blocks, 'cols', axis=1, tiled=True)]
    dot_general x8, matrix products: 61.8 us -> 36 us  [local(): jnp.dot(inverse_full[block_index], pushed, precision=HIGHEST_PRECISION, p...]
    slice x0 -> x2, local copies, waits for them, and re-layouts: none -> 12.2 us  [the longest x1 11.1 us: local(): coupling_full[block_index]]
    another operation x0 -> x1, local copies, waits for them, and re-layouts: none -> 6.15 us  [place_sources_all(): x_now = jnp.tile(message, xs_all)]
    unnamed x33 -> x40, local copies, waits for them, and re-layouts: 1.62 us -> 7.53 us
    all_to_all x0 -> x1, starting transfers between devices: none -> 5.15 us  [place_sources_all(): lax.all_to_all(x_now, 'cols', split_axis=on_dim, concat_axis=on_dim, tile...]
  transfers between devices with their start and end apart: 5 -> 5, of which waited for: 5 -> 4; matrix products, arithmetic and copies ran while one was open for 2% -> 5% of each run, Pallas kernels for 0% -> 0%
where the time goes in v1:
time: 456 us; the launch traced here: 453 us
  waiting for transfers between devices  318 us (70%)
  matrix products  76.7 us (17%)
  local copies, waits for them, and re-layouts  27.7 us (6%)
  between operations  14.3 us (3%)
  starting transfers between devices  13.2 us (3%)
    all_to_all x1, waiting for transfers between devices, place_sources_all(): lax.all_to_all(x_now, 'cols', split_axis=on_dim, concat_axis=on_dim, tile...  246 us
    ppermute x3, waiting for transfers between devices, shifted(): return lax.ppermute(shard, axis, pairs)  72.1 us
    dot_general x8, matrix products, local(): jnp.dot(coupling_full[block_index], previous, precision=HIGHEST_PRECISION...  40.7 us
    dot_general x8, matrix products, local(): jnp.dot(inverse_full[block_index], pushed, precision=HIGHEST_PRECISION, p...  36 us
    slice x1, local copies, waits for them, and re-layouts, local(): coupling_full[block_index]  11.1 us
  transfers between devices with their start and end apart: 5, of which 4 were waited for; matrix products, arithmetic and copies ran while one was open for 5% of the time, Pallas kernels for 0%

profile of v1, /device:TPU:4, one launch (start us, length us, event | category | flops | bytes accessed | tf_op | source)
XLA Modules:
  0.0 452.5 jit_solution(14295156681972195569)
XLA Ops:
  8.6 6.2 %tile.4 = f32[2,8,128,1024]{3,0,2,1:T(2,128)} broadcast(f32[2,128,1024]{2,0,1:T(2,128)S(1)} %copy.17), dimensions={0,2,3} | broadcast | bytes 9437184 | tf_op jit(solution)/shard_map/tile | solution.py:13
  14.7 5.2 %all-to-all-start = ((f32[2,1024,1024]{2,0,1:T(2,128)}), f32[2,1024,1024]{2,0,1:T(2,128)}, u32[]{:S(2)}, u32[]{:S(2)}) async-start(f32[2,1024,1024]{2,0,1:T(2,128)} %bitcast.137), calls=%async_computation | async-start | bytes 16777216 | tf_op jit(solution)/shard_map/all_to_all | solution.py:14
  25.2 245.9 %all-to-all-done = f32[2,1024,1024]{2,0,1:T(2,128)} async-done(((f32[2,1024,1024]{2,0,1:T(2,128)}), f32[2,1024,1024]{2,0,1:T(2,128)}, u32[]{:S(2)}, u32[]{:S(2)}) %all-to-all-start) | async-done | bytes 8388640 | tf_op jit(solution)/shard_map/all_to_all | solution.py:14
  271.2 11.1 %fusion.91 = (f32[1,1024,1024]{2,0,1:T(1,128)}, f32[1,1024,1024]{2,0,1:T(1,128)S(1)}) fusion(f32[2,1024,1024]{2,0,1:T(2,128)} %all-to-all-done), kind=kLoop, calls=%fused_computation.65 | loop fusion | bytes 16777216 | tf_op jit(solution)/shard_map/slice | solution.py:50
  284.2 5.1 %fusion.36 = f32[1024,256]{0,1:T(8,128)} fusion(f32[1024,256]{0,1:T(8,128)S(1)} %copy.24, f32[1,1024,1024]{2,0,1:T(1,128)S(1)} %get-tuple-element.6, f32[1024,256]{0,1:T(8,128)S(1)} %copy.20, pred[]{:T(512)S(6)} %eq.2), kind=kOutput, calls=%fused_computation.40 | convolution fusion | flops 3221749760 | bytes 7340033 | tf_op jit(solution)/shard_map/dot_general | solution.py:49
  289.3 6.1 %fusion.19 = f32[256,1024]{1,0:T(8,128)S(1)} fusion(f32[1024,256]{0,1:T(8,128)} %fusion.36, f32[2,1024,1024]{2,1,0:T(8,128)} %all-gather.2.cloned.1.call-done), kind=kOutput, calls=%fused_computation.21 | convolution fusion | flops 3221225472 | bytes 6291456 | tf_op jit(solution)/shard_map/dot_general | solution.py:55
  295.4 7.6 %fusion.60 = f32[1024,256]{0,1:T(8,128)S(1)} fusion(f32[1024,256]{0,1:T(8,128)S(1)} %copy.25, f32[256,1024]{1,0:T(8,128)S(1)} %fusion.19, f32[1,1024,1024]{2,0,1:T(1,128)} %get-tuple-element.5), kind=kOutput, calls=%fused_computation.48 | convolution fusion | flops 3221487616 | bytes 7340032 | tf_op jit(solution)/shard_map/dot_general | solution.py:49
  303.1 3.7 fusion.23
  306.9 3.4 collective-permute-start
  310.3 24.0 %collective-permute-done = f32[1024,256]{0,1:T(8,128)S(1)} collective-permute-done((f32[1024,256]{0,1:T(8,128)S(1)}, f32[1024,256]{0,1:T(8,128)S(1)}, u32[]{:S(2)}, u32[]{:S(2)}) %collective-permute-start) | collective-permute-done | bytes 1048608 | tf_op jit(solution)/shard_map/ppermute | solution.py:23
  334.3 4.2 fusion.42
  338.5 3.7 fusion.18
  342.2 4.1 fusion.66
  346.3 3.9 fusion.22
  352.8 24.0 %collective-permute-done.1 = f32[1024,256]{0,1:T(8,128)S(1)} collective-permute-done((f32[1024,256]{0,1:T(8,128)S(1)}, f32[1024,256]{0,1:T(8,128)S(1)}, u32[]{:S(2)}, u32[]{:S(2)}) %collective-permute-start.1) | collective-permute-done | bytes 1048608 | tf_op jit(solution)/shard_map/ppermute | solution.py:23
  376.8 4.2 fusion.48
  381.0 3.7 fusion.17
  384.8 4.1 fusion.72
  388.9 4.9 %fusion.21 = f32[256,1024]{1,0:T(8,128)} fusion(f32[1024,256]{0,1:T(8,128)S(1)} %fusion.72, f32[2,1024,1024]{2,1,0:T(8,128)S(1)} %copy-done), kind=kOutput, calls=%fused_computation.23 | convolution fusion | flops 3221225472 | bytes 6291456 | tf_op jit(solution)/shard_map/dot_general | solution.py:55
  395.7 24.0 %collective-permute-done.2 = f32[1024,256]{0,1:T(8,128)} collective-permute-done((f32[1024,256]{0,1:T(8,128)}, f32[1024,256]{0,1:T(8,128)}, u32[]{:S(2)}, u32[]{:S(2)}) %collective-permute-start.2) | collective-permute-done | bytes 1048608 | tf_op jit(solution)/shard_map/ppermute | solution.py:23
  419.8 7.3 %fusion.54 = f32[1024,256]{0,1:T(8,128)S(1)} fusion(f32[1024,256]{0,1:T(8,128)S(1)} %copy.24, f32[1,1024,1024]{2,0,1:T(1,128)} %copy-done.3, f32[1024,256]{0,1:T(8,128)S(1)} %copy.20, f32[1024,256]{0,1:T(8,128)} %collective-permute-done.2, pred[]{:T(512)S(6)} %eq.2), kind=kOutput, calls=%fused_computation.46 | convolution fusion | flops 3221749760 | bytes 8388609 | tf_op jit(solution)/shard_map/dot_general | solution.py:49
  427.0 6.1 %fusion.16 = f32[256,1024]{1,0:T(8,128)S(1)} fusion(f32[1024,256]{0,1:T(8,128)S(1)} %fusion.54, f32[2,1024,1024]{2,1,0:T(8,128)} %all-gather.2.cloned.1.call-done), kind=kOutput, calls=%fused_computation.18 | convolution fusion | flops 3221225472 | bytes 6291456 | tf_op jit(solution)/shard_map/dot_general | solution.py:55
  433.2 4.1 fusion.78
  437.4 3.8 fusion.32
  (49 shorter events, 17.8 us)
Async XLA Ops:
  14.7 5.9 %copy-start.15 = (f32[2048,256]{1,0:T(8,128)S(1)}, f32[2048,256]{1,0:T(8,128)}, u32[]{:S(2)}) copy-start(f32[2048,256]{1,0:T(8,128)} %param.4) | copy-start | bytes 6291460
  14.7 256.4 %all-to-all-start = ((f32[2,1024,1024]{2,0,1:T(2,128)}), f32[2,1024,1024]{2,0,1:T(2,128)}, u32[]{:S(2)}, u32[]{:S(2)}) async-start(f32[2,1024,1024]{2,0,1:T(2,128)} %bitcast.137), calls=%async_computation | async-start | bytes 16777216 | tf_op jit(solution)/shard_map/all_to_all | solution.py:14
  19.9 269.4 %all-gather.2.cloned.1.call-start = ((), (), s32[]{:S(2)}) async-start(), calls=%async_computation.1 | async-start | bytes 9437184 | tf_op jit(solution)/shard_map/all_gather | solution.py:34
  282.3 2.0 copy-start.3
  289.3 13.8 %copy-start = (f32[2,1024,1024]{2,1,0:T(8,128)S(1)}, f32[2,1024,1024]{2,1,0:T(8,128)}, u32[]{:S(2)}) copy-start(f32[2,1024,1024]{2,1,0:T(8,128)} %all-gather.2.cloned.1.call-done) | copy-start | bytes 25165828
  295.4 11.4 %copy-start.5 = (f32[256,1024]{1,0:T(8,128)}, f32[256,1024]{1,0:T(8,128)S(1)}, u32[]{:S(2)}) copy-start(f32[256,1024]{1,0:T(8,128)S(1)} %fusion.19) | copy-start | bytes 3145732
  303.1 31.2 %copy-start.4 = (f32[1,1024,1024]{2,0,1:T(1,128)S(1)}, f32[1,1024,1024]{2,0,1:T(1,128)}, u32[]{:S(2)}) copy-start(f32[1,1024,1024]{2,0,1:T(1,128)} %copy-done.3) | copy-start | bytes 12582916
  306.8 27.4 %copy-start.11 = (f32[256,1024]{1,0:T(8,128)}, f32[256,1024]{1,0:T(8,128)S(1)}, u32[]{:S(2)}) copy-start(f32[256,1024]{1,0:T(8,128)S(1)} %fusion.23) | copy-start | bytes 3145732
  306.9 27.4 %collective-permute-start = (f32[1024,256]{0,1:T(8,128)S(1)}, f32[1024,256]{0,1:T(8,128)S(1)}, u32[]{:S(2)}, u32[]{:S(2)}) collective-permute-start(f32[1024,256]{0,1:T(8,128)S(1)} %bitcast.142), channel_id=1, source_target_pairs={{0,8},{8,16},{16,24},{1,9},{9,17},{17,25},{2,10},{10,18},{18,26},{... | collective-permute-start | bytes 3145736 | tf_op jit(solution)/shard_map/ppermute | solution.py:23
  338.4 3.8 copy-start.1
  342.2 8.0 %copy-start.7 = (f32[256,1024]{1,0:T(8,128)}, f32[256,1024]{1,0:T(8,128)S(1)}, u32[]{:S(2)}) copy-start(f32[256,1024]{1,0:T(8,128)S(1)} %fusion.18) | copy-start | bytes 3145732
  350.3 30.7 %copy-start.13 = (f32[256,1024]{1,0:T(8,128)}, f32[256,1024]{1,0:T(8,128)S(1)}, u32[]{:S(2)}) copy-start(f32[256,1024]{1,0:T(8,128)S(1)} %fusion.22) | copy-start | bytes 3145732
  350.3 26.5 %collective-permute-start.1 = (f32[1024,256]{0,1:T(8,128)S(1)}, f32[1024,256]{0,1:T(8,128)S(1)}, u32[]{:S(2)}, u32[]{:S(2)}) collective-permute-start(f32[1024,256]{0,1:T(8,128)S(1)} %bitcast.144), channel_id=1, source_target_pairs={{0,8},{8,16},{16,24},{1,9},{9,17},{17,25},{2,10},{10,18},{18,26},{... | collective-permute-start | bytes 3145736 | tf_op jit(solution)/shard_map/ppermute | solution.py:23
  384.7 9.0 %copy-start.9 = (f32[256,1024]{1,0:T(8,128)}, f32[256,1024]{1,0:T(8,128)S(1)}, u32[]{:S(2)}) copy-start(f32[256,1024]{1,0:T(8,128)S(1)} %fusion.17) | copy-start | bytes 3145732
  393.8 26.0 %collective-permute-start.2 = (f32[1024,256]{0,1:T(8,128)}, f32[1024,256]{0,1:T(8,128)}, u32[]{:S(2)}, u32[]{:S(2)}) collective-permute-start(f32[1024,256]{0,1:T(8,128)} %bitcast.11), channel_id=1, source_target_pairs={{0,8},{8,16},{16,24},{1,9},{9,17},{17,25},{2,10},{10,18},{18,26},{... | collective-permute-start | bytes 3145736 | tf_op jit(solution)/shard_map/ppermute | solution.py:23
  419.8 13.4 %copy-start.2 = (f32[1,1024,1024]{2,0,1:T(1,128)S(1)}, f32[1,1024,1024]{2,0,1:T(1,128)}, u32[]{:S(2)}) copy-start(f32[1,1024,1024]{2,0,1:T(1,128)} %get-tuple-element.5) | copy-start | bytes 12582916
  419.8 17.6 %slice-start = ((s8[8388608]{0:T(1024)(128)(4,1)}), s8[4194304]{0:T(1024)(128)(4,1)S(1)}, s32[]{:S(2)}) async-start(s8[8388608]{0:T(1024)(128)(4,1)} %bitcast.135), calls=%async_computation.2 | async-start | bytes 8388608
  427.0 10.3 %slice-start.1 = ((s8[8388608]{0:T(1024)(128)(4,1)}), s8[4194304]{0:T(1024)(128)(4,1)S(1)}, s32[]{:S(2)}) async-start(s8[8388608]{0:T(1024)(128)(4,1)} %bitcast.135), calls=%async_computation.3 | async-start | bytes 8388608
  437.4 3.8 copy-start.6
  437.4 3.8 copy-start.8
  437.4 3.8 copy-start.10
  437.4 3.8 copy-start.12
  437.4 3.8 copy-start.14
Sparse Core Ops, SparseCore 0:
  22.3 152.0 all-gather.1
